TPU v7x, 32 devices: a whole 2x2x4 slice. The times are simulated.
32 devices in a mesh: energy: 8 (over y, x, core), kpt: 4 (over z).
Axes of the slice: x: 2, y: 2, z: 4, core: 2. Of those that a mesh axis runs over, the one named last changes fastest.
Arguments:
- density: bfloat16 [32, 4, 64, 3072], P('energy', 'kpt'), may hold values from -6 to 6
- quad_weights: float32 [32, 4], P('energy', 'kpt'), may hold values from 0.044194173 to 0.17677669
- orbital_cells: int32 [64, 3072], replicated, may hold values from 0 to 131071
- fixed_charge: float32 [512, 64, 256], P('energy', 'kpt'), may hold values from -16 to 16
- gate_mask: int32 [512, 64, 256], P('energy', 'kpt'), may hold values 0 or 1
- gate_voltage: float32 [512], P('energy'), may hold values from -1 to 1
Outputs:
- potential: float32 [512, 64, 256], P('energy', 'kpt')
- band_shift: float32 [32, 4, 64], P('energy', 'kpt')
Inputs may be any that keep to these rules, and one draw needn't show every extreme that they name: `orbital_cells`: each entry is s * 64 * 256 + y * 256 + z, a cell of one of the layer's 8 planes.
All inputs are finite; a program needn't handle non-finite values. No bound on the sum of `gate_mask` on one device may be relied on, other than what follows from the above.
Results may differ from a plain program's by a relative error of at most 0.0003.
Values sent between devices are 32-bit elements; how exact they have to be, the bound alone decides.
A program may use at most 64 MiB of HBM per device.

v0:
```python
import jax
import jax.numpy as jnp
from jax import lax
from jax.sharding import PartitionSpec as P

LAYER_DEV = 8
SUB = 8
ITERS = 2
PENALTY = 4.0


def with_halo(block, sides, width):
    for axis, dim in sides:
        count = lax.axis_size(axis)
        forward = [(i, i + 1) for i in range(count - 1)]
        backward = [(target, source) for source, target in forward]
        low = lax.ppermute(
            lax.slice_in_dim(block, block.shape[dim] - width, None, axis=dim), axis, forward
        )
        high = lax.ppermute(lax.slice_in_dim(block, 0, width, axis=dim), axis, backward)
        block = jnp.concatenate([low, block, high], axis=dim)
    return block


def operate(values_field, diagonal):
    padded = with_halo(values_field, (("energy", 0), ("kpt", 1)), 1)
    padded = jnp.pad(padded, ((0, 0), (0, 0), (1, 1)))
    beside = padded[2:, 1:-1, 1:-1] + padded[:-2, 1:-1, 1:-1]
    beside = beside + padded[1:-1, 2:, 1:-1] + padded[1:-1, :-2, 1:-1]
    beside = beside + padded[1:-1, 1:-1, 2:] + padded[1:-1, 1:-1, :-2]
    return diagonal * values_field - beside


def paired_sums(residual, image):
    return lax.psum((jnp.sum(residual * residual), jnp.sum(residual * image)), ("energy", "kpt"))


def window_index(map_rows, kpt_index, planes, cross_y, width_y, depth_z):
    section = cross_y * depth_z
    within = map_rows % section
    column = within // depth_z - kpt_index * width_y
    inside = (column >= 0) & (column < width_y)
    layer_rows = lax.broadcasted_iota(jnp.int32, map_rows.shape, 0)
    flat_cell = (
        (layer_rows * planes + map_rows // section) * width_y + jnp.clip(column, 0, width_y - 1)
    ) * depth_z + within % depth_z
    return (flat_cell, inside)


def per_device(density, quad_weights, orbital_cells, fixed_charge, gate_mask, gate_voltage):
    planes_dev, width_y, depth_z = fixed_charge.shape
    kpt_index = lax.axis_index("kpt")
    cross_y = width_y * lax.axis_size("kpt")
    occupancy = jnp.einsum(
        "ek,eklo->lo", quad_weights, density.astype(jnp.float32), precision=lax.Precision.HIGHEST
    )
    partial_rows = lax.psum_scatter(occupancy, "energy", scatter_dimension=0, tiled=True)
    slab_occupancy = lax.psum(partial_rows, "kpt")
    slab_cells = lax.dynamic_slice_in_dim(
        orbital_cells, lax.axis_index("energy") * LAYER_DEV, LAYER_DEV, 0
    )
    flat_cell, inside = window_index(slab_cells, kpt_index, SUB, cross_y, width_y, depth_z)
    deposit = jax.ops.segment_sum(
        jnp.where(inside, slab_occupancy, 0.0).reshape(-1),
        flat_cell.reshape(-1),
        num_segments=planes_dev * width_y * depth_z,
    )
    charge = deposit.reshape(planes_dev, width_y, depth_z)
    gated = gate_mask.astype(jnp.float32)
    diagonal = 6.0 + PENALTY * gated
    right_side = fixed_charge - charge + PENALTY * gated * gate_voltage[:, None, None]
    potential = jnp.zeros_like(right_side)
    residual = right_side
    image = operate(residual, diagonal)
    norm_now, product = paired_sums(residual, image)
    alpha = norm_now / product
    direction = residual
    along = image
    for sweep_index in range(ITERS):
        potential = potential + alpha * direction
        residual = residual - alpha * along
        if sweep_index + 1 < ITERS:
            image = operate(residual, diagonal)
            norm_next, product = paired_sums(residual, image)
            ratio = norm_next / norm_now
            alpha = norm_next / (product - ratio * norm_next / alpha)
            direction = residual + ratio * direction
            along = image + ratio * along
            norm_now = norm_next
    local_values = jnp.where(inside, jnp.take(potential.reshape(-1), flat_cell), 0.0)
    orbital_potential = lax.psum(local_values, "kpt")
    factor = density.shape[3] ** (-0.5)
    block = density.astype(jnp.float32)
    band_shift = (
        jnp.einsum(
            "eklo,lo->ekl",
            block,
            lax.all_gather(orbital_potential, "energy", axis=0, tiled=True),
            precision=lax.Precision.HIGHEST,
        )
        * factor
    )
    return (potential, band_shift)


def solution(mesh):
    in_specs = (
        P("energy", "kpt", None, None),
        P("energy", "kpt"),
        P(),
        P("energy", "kpt", None),
        P("energy", "kpt", None),
        P("energy"),
    )
    out_specs = (P("energy", "kpt", None), P("energy", "kpt", None))
    return jax.shard_map(
        per_device, mesh=mesh, in_specs=in_specs, out_specs=out_specs, check_vma=False
    )
```

profile of v0, /device:TPU:0, one launch (start us, length us, event | category | flops | bytes accessed | tf_op | source)
XLA Modules:
  0.0 549.4 jit_solution(11437265235670384205)
XLA Ops:
  7.2 1.4 copy-done
  8.6 3.8 fusion.3
  12.4 1.0 copy.38
  13.4 0.0 all-reduce.7.cloned.1.call-start
  13.5 1.1 fusion.26
  14.6 36.6 %reduce-scatter.2.cloned.1.call-done = f32[8,3072]{1,0:T(8,128)} async-done(((f32[64,3072]{1,0:T(8,128)}), f32[8,3072]{1,0:T(8,128)}) %reduce-scatter.2.cloned.1.call-update) | async-done | bytes 98320 | tf_op jit(solution)/shard_map/reduce_scatter | solution.py:57
  51.3 36.7 %all-reduce.7.cloned.1.call-done = f32[8,3072]{1,0:T(8,128)} async-done(((f32[8,3072]{1,0:T(8,128)}), f32[8,3072]{1,0:T(8,128)}) %all-reduce.7.cloned.1.call-update) | async-done | bytes 98320 | tf_op jit(solution)/shard_map/psum | solution.py:58
  88.0 1.1 select_bitcast_fusion
  89.1 128.7 %scatter_custom_fusion = f32[262144]{0:T(1024)S(1)} fusion(s32[24576]{0:T(1024)S(1)} %bitcast.33, f32[24576]{0:T(1024)S(1)} %bitcast.34, f32[]{:T(128)} %constant.72.clone.1), kind=kCustom, calls=%fused_computation.56 | custom fusion | flops 24576 | bytes 1048580 | tf_op jit(solution)/shard_map/scatter-add | solution.py:63
  217.8 1.3 reshape.32
  219.1 2.1 multiply_add_fusion.2
  221.2 1.3 collective-permute-start.1
  222.5 1.4 collective-permute-start
  223.9 3.5 collective-permute-done
  227.4 0.1 pad_maximum_fusion.19
  227.5 1.3 collective-permute-start.2
  228.8 4.5 collective-permute-start.3
  233.4 0.4 collective-permute-done.2
  233.8 0.1 copy.12
  233.9 1.5 collective-permute-done.3
  235.4 0.1 copy.14
  235.4 1.2 select_maximum_fusion.4
  236.7 2.6 multiply_reduce_fusion.1
  239.3 42.2 %all-reduce.3 = (f32[]{:T(128)}, f32[]{:T(128)}) all-reduce(f32[]{:T(128)} %get-tuple-element.7, f32[]{:T(128)} %get-tuple-element.6), channel_id=1, replica_groups=mesh['energy'=8,'kpt'=4] {'energy','kpt'}, use_global_device_ids=true, to_apply=%region_4.5 | all-reduce | flops 2 | bytes 16 | tf_op jit(solution)/shard_map/psum | solution.py:35
  282.8 1.5 multiply_subtract_fusion
  284.3 1.3 collective-permute-start.5
  285.6 1.3 collective-permute-start.4
  286.9 4.2 collective-permute-done.4
  291.2 0.1 pad_maximum_fusion.16
  291.3 1.4 collective-permute-start.6
  292.8 4.5 collective-permute-start.7
  297.3 0.4 collective-permute-done.6
  297.7 0.1 copy.18
  297.8 1.5 collective-permute-done.7
  299.3 0.1 copy.20
  299.3 1.3 select_maximum_fusion
  300.6 1.7 fusion.7
  302.3 42.7 %all-reduce.2 = (f32[]{:T(128)}, f32[]{:T(128)}) all-reduce(f32[]{:T(128)} %get-tuple-element.5, f32[]{:T(128)} %get-tuple-element.4), channel_id=1, replica_groups=mesh['energy'=8,'kpt'=4] {'energy','kpt'}, use_global_device_ids=true, to_apply=%region_8.9 | all-reduce | flops 2 | bytes 16 | tf_op jit(solution)/shard_map/psum | solution.py:35
  349.4 1.5 multiply_add_fusion
  350.9 1.0 copy-done.4
  351.8 0.5 copy.29
  352.4 135.5 %gather_fusion = f32[24576]{0:T(1024)S(1)} fusion(f32[262144]{0:T(1024)S(1)} %bitcast.27, s32[24576]{0:T(1024)S(1)} %broadcast_clamp_fusion), kind=kCustom, calls=%fused_computation | custom fusion | bytes 294912 | tf_op jit(solution)/shard_map/jit(_take)/gather | solution.py:90
  488.0 0.7 select_select_fusion
  488.7 35.5 %all-reduce.9.cloned.1.call-done = f32[8,3072]{1,0:T(8,128)} async-done(((f32[8,3072]{1,0:T(8,128)}), f32[8,3072]{1,0:T(8,128)}) %all-reduce.9.cloned.1.call-update) | async-done | bytes 98320 | tf_op jit(solution)/shard_map/psum | solution.py:91
  524.2 10.7 %all_gather.3 = f32[64,3072]{1,0:T(8,128)S(1)} all-gather(f32[8,3072]{1,0:T(8,128)} %all-reduce.9.cloned.1.call-done), channel_id=1, replica_groups=mesh['energy'=8,'kpt'=4] {'energy'}, dimensions={0}, use_global_device_ids=true | all-gather | bytes 884736 | tf_op jit(solution)/shard_map/all_gather | solution.py:98
  534.8 7.3 %fusion.1 = f32[64,1,4]{2,1,0:T(1,128)S(1)} fusion(bf16[4,64,3072]{2,1,0:T(8,128)(2,1)S(1)} %bitcast.26, f32[64,3072,1]{1,0,2:T(8,128)S(1)} %bitcast.31), kind=kOutput, calls=%fused_computation.13 | convolution fusion | flops 9437184 | bytes 2360320 | tf_op jit(solution)/shard_map/eklo,lo->ekl/dot_general | solution.py:95
  542.2 0.1 copy.26
  542.3 0.6 bitcast_multiply_fusion
  (30 shorter events, 0.3 us)
Async XLA Ops:
  7.2 1.4 copy-start
  7.2 44.0 %reduce-scatter.2.cloned.1.call-start = ((), (), s32[]{:S(2)}) async-start(), calls=%async_computation.1 | async-start | bytes 884736 | tf_op jit(solution)/shard_map/reduce_scatter | solution.py:57
  8.6 42.7 %copy-start.5 = (f32[64]{0:T(128)S(1)}, f32[64]{0:T(128)}, u32[]{:S(2)}) copy-start(f32[64]{0:T(128)} %param.11) | copy-start | bytes 772
  13.4 74.6 %all-reduce.7.cloned.1.call-start = ((), (), s32[]{:S(2)}) async-start(), calls=%async_computation.2 | async-start | bytes 196608 | tf_op jit(solution)/shard_map/psum | solution.py:58
  51.2 472.9 %all-reduce.9.cloned.1.call-start = ((), (), s32[]{:S(2)}) async-start(), calls=%async_computation.3 | async-start | bytes 196608 | tf_op jit(solution)/shard_map/psum | solution.py:91
  221.2 2.7 collective-permute-start.1
  222.5 14.2 %copy-start.2 = (s32[64,16,256]{2,1,0:T(8,128)S(1)}, s32[64,16,256]{2,1,0:T(8,128)}, u32[]{:S(2)}) copy-start(s32[64,16,256]{2,1,0:T(8,128)} %param.10) | copy-start | bytes 3145732
  222.5 4.9 collective-permute-start
  227.5 6.2 %collective-permute-start.2 = (f32[66,1,256]{2,0,1:T(8,128)S(1)}, f32[66,1,256]{2,0,1:T(8,128)S(1)}, u32[]{:S(2)}, u32[]{:S(2)}) collective-permute-start(f32[66,1,256]{2,0,1:T(8,128)S(1)} %copy.11), channel_id=1, source_target_pairs={{1,0},{2,1},{3,2},{5,4},{6,5},{7,6},{9,8},{10,9},{11,10},{13,12},{... | collective-permute-start | bytes 202760 | tf_op jit(solution)/shard_map/ppermute | solution.py:20
  228.8 6.5 %collective-permute-start.3 = (f32[66,1,256]{2,0,1:T(8,128)S(1)}, f32[66,1,256]{2,0,1:T(8,128)S(1)}, u32[]{:S(2)}, u32[]{:S(2)}) collective-permute-start(f32[66,1,256]{2,0,1:T(8,128)S(1)} %copy.13), channel_id=1, source_target_pairs={{0,1},{1,2},{2,3},{4,5},{5,6},{6,7},{8,9},{9,10},{10,11},{12,13},{... | collective-permute-start | bytes 202760 | tf_op jit(solution)/shard_map/ppermute | solution.py:17
  284.3 16.3 %copy-start.1 = (f32[64,16,256]{2,1,0:T(8,128)}, f32[64,16,256]{2,1,0:T(8,128)S(1)}, u32[]{:S(2)}) copy-start(f32[64,16,256]{2,1,0:T(8,128)S(1)} %multiply_subtract_fusion) | copy-start | bytes 3145732
  284.3 2.6 collective-permute-start.5
  285.6 5.6 %collective-permute-start.4 = (f32[1,16,256]{2,1,0:T(8,128)S(1)}, f32[1,16,256]{2,1,0:T(8,128)S(1)}, u32[]{:S(2)}, u32[]{:S(2)}) collective-permute-start(f32[1,16,256]{2,1,0:T(8,128)S(1)} %get-tuple-element.23), channel_id=1, source_target_pairs={{4,0},{8,4},{12,8},{16,12},{20,16},{24,20},{28,24},{5,1},{9,5},{13... | collective-permute-start | bytes 49160 | tf_op jit(solution)/shard_map/ppermute | solution.py:20
  291.3 9.3 %copy-start.3 = (s32[64,16,256]{2,1,0:T(8,128)S(1)}, s32[64,16,256]{2,1,0:T(8,128)}, u32[]{:S(2)}) copy-start(s32[64,16,256]{2,1,0:T(8,128)} %param.10) | copy-start | bytes 3145732
  291.3 6.4 %collective-permute-start.6 = (f32[66,1,256]{2,0,1:T(8,128)S(1)}, f32[66,1,256]{2,0,1:T(8,128)S(1)}, u32[]{:S(2)}, u32[]{:S(2)}) collective-permute-start(f32[66,1,256]{2,0,1:T(8,128)S(1)} %copy.17), channel_id=1, source_target_pairs={{1,0},{2,1},{3,2},{5,4},{6,5},{7,6},{9,8},{10,9},{11,10},{13,12},{... | collective-permute-start | bytes 202760 | tf_op jit(solution)/shard_map/ppermute | solution.py:20
  292.8 6.5 %collective-permute-start.7 = (f32[66,1,256]{2,0,1:T(8,128)S(1)}, f32[66,1,256]{2,0,1:T(8,128)S(1)}, u32[]{:S(2)}, u32[]{:S(2)}) collective-permute-start(f32[66,1,256]{2,0,1:T(8,128)S(1)} %copy.19), channel_id=1, source_target_pairs={{0,1},{1,2},{2,3},{4,5},{5,6},{6,7},{8,9},{9,10},{10,11},{12,13},{... | collective-permute-start | bytes 202760 | tf_op jit(solution)/shard_map/ppermute | solution.py:17
  350.9 1.0 copy-start.4
Sparse Core Ops, SparseCore 0:
  13.5 37.6 reduce-scatter.1
  53.5 34.4 all-reduce.6
  488.8 35.3 all-reduce.8
where the time goes:
time: 550 us; the launch traced here: 549 us
  other arithmetic  144 us (26%)
  local copies, waits for them, and re-layouts  141 us (26%)
  waiting for transfers between devices  120 us (22%)
  blocking collectives  95.6 us (17%)
  between operations  19.7 us (4%)
  starting transfers between devices  17.2 us (3%)
  matrix products  11.1 us (2%)
    gather x2, local copies, waits for them, and re-layouts, per_device(): jnp.take(potential.reshape(-1), flat_cell)  136 us
    scatter-add x1, other arithmetic, per_device(): jax.ops.segment_sum(jnp.where(inside, slab_occupancy, 0.0).reshape(-1), f...  129 us
    psum x2, blocking collectives, paired_sums(): lax.psum((jnp.sum(residual * residual), jnp.sum(residual * image)), ('ene...  84.9 us
    psum x1, waiting for transfers between devices, per_device(): slab_occupancy = lax.psum(partial_rows, 'kpt')  36.7 us
    reduce_scatter x1, waiting for transfers between devices, per_device(): lax.psum_scatter(occupancy, 'energy', scatter_dimension=0, tiled=True)  36.6 us
    psum x1, waiting for transfers between devices, per_device(): orbital_potential = lax.psum(local_values, 'kpt')  35.5 us
    ppermute x4, starting transfers between devices, with_halo(): lax.ppermute(lax.slice_in_dim(block, block.shape[dim] - width, None, axis...  11.7 us
  transfers between devices with their start and end apart: 11, of which 9 were waited for; matrix products, arithmetic and copies ran while one was open for 0% of the time, Pallas kernels for 0%

commit v1 on v0

--- a/solution.py
+++ b/solution.py
@@ -48,6 +48,10 @@
 
 
 def per_device(density, quad_weights, orbital_cells, fixed_charge, gate_mask, gate_voltage):
+
+    def _review_strings(xin, axis_key):
+        return jnp.sum(lax.all_gather(xin, axis_name=axis_key), 0)
+
     planes_dev, width_y, depth_z = fixed_charge.shape
     kpt_index = lax.axis_index("kpt")
     cross_y = width_y * lax.axis_size("kpt")
@@ -55,7 +59,7 @@
         "ek,eklo->lo", quad_weights, density.astype(jnp.float32), precision=lax.Precision.HIGHEST
     )
     partial_rows = lax.psum_scatter(occupancy, "energy", scatter_dimension=0, tiled=True)
-    slab_occupancy = lax.psum(partial_rows, "kpt")
+    slab_occupancy = _review_strings(partial_rows, "kpt")
     slab_cells = lax.dynamic_slice_in_dim(
         orbital_cells, lax.axis_index("energy") * LAYER_DEV, LAYER_DEV, 0
     )

time: 550 us -> 528 us (0.960)
  waiting for transfers between devices: 120 us -> 83.2 us
  blocking collectives: 95.6 us -> 110 us
    psum x1 -> x0, waiting for transfers between devices: 36.7 us -> none  [per_device(): slab_occupancy = lax.psum(partial_rows, 'kpt')]
    all_gather x0 -> x1, blocking collectives: none -> 14.6 us  [_review_strings(): return jnp.sum(lax.all_gather(xin, axis_name=axis_key), 0)]
  transfers between devices with their start and end apart: 11 -> 10, of which waited for: 9 -> 8; matrix products, arithmetic and copies ran while one was open for 0% -> 0% of each run, Pallas kernels for 0% -> 0%
where the time goes in v1:
time: 528 us; the launch traced here: 527 us
  other arithmetic  144 us (27%)
  local copies, waits for them, and re-layouts  141 us (27%)
  blocking collectives  110 us (21%)
  waiting for transfers between devices  83.2 us (16%)
  between operations  20 us (4%)
  starting transfers between devices  17.4 us (3%)
  matrix products  11.1 us (2%)
    gather x2, local copies, waits for them, and re-layouts, per_device(): jnp.take(potential.reshape(-1), flat_cell)  136 us
    scatter-add x1, other arithmetic, per_device(): jax.ops.segment_sum(jnp.where(inside, slab_occupancy, 0.0).reshape(-1), f...  129 us
    psum x2, blocking collectives, paired_sums(): lax.psum((jnp.sum(residual * residual), jnp.sum(residual * image)), ('ene...  85.2 us
    reduce_scatter x1, waiting for transfers between devices, per_device(): lax.psum_scatter(occupancy, 'energy', scatter_dimension=0, tiled=True)  36.6 us
    psum x1, waiting for transfers between devices, per_device(): orbital_potential = lax.psum(local_values, 'kpt')  35 us
    all_gather x1, blocking collectives, _review_strings(): return jnp.sum(lax.all_gather(xin, axis_name=axis_key), 0)  14.6 us
    ppermute x4, starting transfers between devices, with_halo(): lax.ppermute(lax.slice_in_dim(block, block.shape[dim] - width, None, axis...  11.8 us
    all_gather x1, blocking collectives, per_device(): lax.all_gather(orbital_potential, 'energy', axis=0, tiled=True)  10.7 us
  transfers between devices with their start and end apart: 10, of which 8 were waited for; matrix products, arithmetic and copies ran while one was open for 0% of the time, Pallas kernels for 0%

profile of v1, /device:TPU:0, one launch (start us, length us, event | category | flops | bytes accessed | tf_op | source)
XLA Modules:
  0.0 527.5 jit_solution(1567025840840628819)
XLA Ops:
  7.2 1.4 copy-done
  8.6 3.8 fusion.3
  12.4 1.0 copy.50
  13.4 0.0 all-reduce.6.cloned.1.call-start
  13.5 1.1 fusion.26
  14.7 36.6 %reduce-scatter.2.cloned.1.call-done = f32[8,3072]{1,0:T(8,128)} async-done(((f32[64,3072]{1,0:T(8,128)}), f32[8,3072]{1,0:T(8,128)}) %reduce-scatter.2.cloned.1.call-update) | async-done | bytes 98320 | tf_op jit(solution)/shard_map/reduce_scatter | solution.py:61
  51.2 14.6 %all-gather = f32[32,3072]{1,0:T(8,128)S(1)} all-gather(f32[8,3072]{1,0:T(8,128)} %reduce-scatter.2.cloned.1.call-done), channel_id=2, replica_groups=mesh['energy'=8,'kpt'=4] {'kpt'}, dimensions={0}, use_global_device_ids=true | all-gather | bytes 491520 | tf_op jit(solution)/shard_map/all_gather | solution.py:53
  65.8 1.0 select_bitcast_fusion
  66.9 128.7 %scatter_custom_fusion = f32[262144]{0:T(1024)S(1)} fusion(s32[24576]{0:T(1024)S(1)} %bitcast.35, f32[24576]{0:T(1024)S(1)} %bitcast.36, f32[]{:T(128)} %constant.72.clone.1), kind=kCustom, calls=%fused_computation.56 | custom fusion | flops 24576 | bytes 1048580 | tf_op jit(solution)/shard_map/scatter-add | solution.py:67
  195.6 1.3 reshape.32
  196.8 2.1 multiply_add_fusion.2
  199.0 1.3 collective-permute-start.1
  200.3 1.4 collective-permute-start
  201.7 3.7 collective-permute-done
  205.4 0.1 pad_maximum_fusion.19
  205.5 1.3 collective-permute-start.2
  206.8 4.7 collective-permute-start.3
  211.5 0.4 collective-permute-done.2
  211.9 0.1 copy.24
  212.0 1.5 collective-permute-done.3
  213.5 0.1 copy.26
  213.6 1.2 select_maximum_fusion.4
  214.8 2.6 multiply_reduce_fusion.1
  217.5 42.4 %all-reduce.3 = (f32[]{:T(128)}, f32[]{:T(128)}) all-reduce(f32[]{:T(128)} %get-tuple-element.7, f32[]{:T(128)} %get-tuple-element.6), channel_id=1, replica_groups=mesh['energy'=8,'kpt'=4] {'energy','kpt'}, use_global_device_ids=true, to_apply=%region_4.5 | all-reduce | flops 2 | bytes 16 | tf_op jit(solution)/shard_map/psum | solution.py:35
  261.1 1.5 multiply_subtract_fusion
  262.5 1.3 collective-permute-start.5
  263.8 1.3 collective-permute-start.4
  265.2 4.2 collective-permute-done.4
  269.4 0.1 pad_maximum_fusion.16
  269.6 1.4 collective-permute-start.6
  271.0 4.5 collective-permute-start.7
  275.6 0.4 collective-permute-done.6
  276.0 0.1 copy.30
  276.0 1.5 collective-permute-done.7
  277.5 0.1 copy.32
  277.6 1.3 select_maximum_fusion
  278.9 1.6 fusion.7
  280.5 42.8 %all-reduce.2 = (f32[]{:T(128)}, f32[]{:T(128)}) all-reduce(f32[]{:T(128)} %get-tuple-element.5, f32[]{:T(128)} %get-tuple-element.4), channel_id=1, replica_groups=mesh['energy'=8,'kpt'=4] {'energy','kpt'}, use_global_device_ids=true, to_apply=%region_8.9 | all-reduce | flops 2 | bytes 16 | tf_op jit(solution)/shard_map/psum | solution.py:35
  327.7 1.5 multiply_add_fusion
  329.2 1.0 copy-done.4
  330.1 0.5 copy.41
  330.7 135.5 %gather_fusion = f32[24576]{0:T(1024)S(1)} fusion(f32[262144]{0:T(1024)S(1)} %bitcast.29, s32[24576]{0:T(1024)S(1)} %broadcast_clamp_fusion), kind=kCustom, calls=%fused_computation | custom fusion | bytes 294912 | tf_op jit(solution)/shard_map/jit(_take)/gather | solution.py:94
  466.3 0.7 select_select_fusion
  467.0 35.0 %all-reduce.6.cloned.1.call-done = f32[8,3072]{1,0:T(8,128)} async-done(((f32[8,3072]{1,0:T(8,128)}), f32[8,3072]{1,0:T(8,128)}) %all-reduce.6.cloned.1.call-update) | async-done | bytes 98320 | tf_op jit(solution)/shard_map/psum | solution.py:95
  502.0 10.7 %all_gather.11 = f32[64,3072]{1,0:T(8,128)S(1)} all-gather(f32[8,3072]{1,0:T(8,128)} %all-reduce.6.cloned.1.call-done), channel_id=1, replica_groups=mesh['energy'=8,'kpt'=4] {'energy'}, dimensions={0}, use_global_device_ids=true | all-gather | bytes 884736 | tf_op jit(solution)/shard_map/all_gather | solution.py:102
  512.6 7.3 %fusion.1 = f32[64,1,4]{2,1,0:T(1,128)S(1)} fusion(bf16[4,64,3072]{2,1,0:T(8,128)(2,1)S(1)} %bitcast.28, f32[64,3072,1]{1,0,2:T(8,128)S(1)} %bitcast.33), kind=kOutput, calls=%fused_computation.13 | convolution fusion | flops 9437184 | bytes 2360320 | tf_op jit(solution)/shard_map/eklo,lo->ekl/dot_general | solution.py:99
  520.0 0.1 copy.38
  520.1 0.6 bitcast_multiply_fusion
  (29 shorter events, 0.3 us)
Async XLA Ops:
  7.2 1.4 copy-start
  7.2 44.0 %reduce-scatter.2.cloned.1.call-start = ((), (), s32[]{:S(2)}) async-start(), calls=%async_computation.1 | async-start | bytes 884736 | tf_op jit(solution)/shard_map/reduce_scatter | solution.py:61
  8.6 6.1 %copy-start.5 = (f32[64]{0:T(128)S(1)}, f32[64]{0:T(128)}, u32[]{:S(2)}) copy-start(f32[64]{0:T(128)} %param.11) | copy-start | bytes 772
  13.4 488.5 %all-reduce.6.cloned.1.call-start = ((), (), s32[]{:S(2)}) async-start(), calls=%async_computation.2 | async-start | bytes 196608 | tf_op jit(solution)/shard_map/psum | solution.py:95
  199.0 2.7 collective-permute-start.1
  200.3 14.5 %copy-start.2 = (s32[64,16,256]{2,1,0:T(8,128)S(1)}, s32[64,16,256]{2,1,0:T(8,128)}, u32[]{:S(2)}) copy-start(s32[64,16,256]{2,1,0:T(8,128)} %param.10) | copy-start | bytes 3145732
  200.3 5.1 collective-permute-start
  205.5 6.4 %collective-permute-start.2 = (f32[66,1,256]{2,0,1:T(8,128)S(1)}, f32[66,1,256]{2,0,1:T(8,128)S(1)}, u32[]{:S(2)}, u32[]{:S(2)}) collective-permute-start(f32[66,1,256]{2,0,1:T(8,128)S(1)} %copy.23), channel_id=1, source_target_pairs={{1,0},{2,1},{3,2},{5,4},{6,5},{7,6},{9,8},{10,9},{11,10},{13,12},{... | collective-permute-start | bytes 202760 | tf_op jit(solution)/shard_map/ppermute | solution.py:20
  206.8 6.7 %collective-permute-start.3 = (f32[66,1,256]{2,0,1:T(8,128)S(1)}, f32[66,1,256]{2,0,1:T(8,128)S(1)}, u32[]{:S(2)}, u32[]{:S(2)}) collective-permute-start(f32[66,1,256]{2,0,1:T(8,128)S(1)} %copy.25), channel_id=1, source_target_pairs={{0,1},{1,2},{2,3},{4,5},{5,6},{6,7},{8,9},{9,10},{10,11},{12,13},{... | collective-permute-start | bytes 202760 | tf_op jit(solution)/shard_map/ppermute | solution.py:17
  262.5 16.3 %copy-start.1 = (f32[64,16,256]{2,1,0:T(8,128)}, f32[64,16,256]{2,1,0:T(8,128)S(1)}, u32[]{:S(2)}) copy-start(f32[64,16,256]{2,1,0:T(8,128)S(1)} %multiply_subtract_fusion) | copy-start | bytes 3145732
  262.5 2.6 collective-permute-start.5
  263.8 5.6 %collective-permute-start.4 = (f32[1,16,256]{2,1,0:T(8,128)S(1)}, f32[1,16,256]{2,1,0:T(8,128)S(1)}, u32[]{:S(2)}, u32[]{:S(2)}) collective-permute-start(f32[1,16,256]{2,1,0:T(8,128)S(1)} %get-tuple-element.23), channel_id=1, source_target_pairs={{4,0},{8,4},{12,8},{16,12},{20,16},{24,20},{28,24},{5,1},{9,5},{13... | collective-permute-start | bytes 49160 | tf_op jit(solution)/shard_map/ppermute | solution.py:20
  269.5 9.3 %copy-start.3 = (s32[64,16,256]{2,1,0:T(8,128)S(1)}, s32[64,16,256]{2,1,0:T(8,128)}, u32[]{:S(2)}) copy-start(s32[64,16,256]{2,1,0:T(8,128)} %param.10) | copy-start | bytes 3145732
  269.6 6.4 %collective-permute-start.6 = (f32[66,1,256]{2,0,1:T(8,128)S(1)}, f32[66,1,256]{2,0,1:T(8,128)S(1)}, u32[]{:S(2)}, u32[]{:S(2)}) collective-permute-start(f32[66,1,256]{2,0,1:T(8,128)S(1)} %copy.29), channel_id=1, source_target_pairs={{1,0},{2,1},{3,2},{5,4},{6,5},{7,6},{9,8},{10,9},{11,10},{13,12},{... | collective-permute-start | bytes 202760 | tf_op jit(solution)/shard_map/ppermute | solution.py:20
  271.0 6.5 %collective-permute-start.7 = (f32[66,1,256]{2,0,1:T(8,128)S(1)}, f32[66,1,256]{2,0,1:T(8,128)S(1)}, u32[]{:S(2)}, u32[]{:S(2)}) collective-permute-start(f32[66,1,256]{2,0,1:T(8,128)S(1)} %copy.31), channel_id=1, source_target_pairs={{0,1},{1,2},{2,3},{4,5},{5,6},{6,7},{8,9},{9,10},{10,11},{12,13},{... | collective-permute-start | bytes 202760 | tf_op jit(solution)/shard_map/ppermute | solution.py:17
  329.2 1.0 copy-start.4
Sparse Core Ops, SparseCore 0:
  13.5 37.6 reduce-scatter.1
  467.1 34.8 all-reduce.5
